TPU v7x, 512 devices: a whole 4x8x8 slice. The times are simulated.
512 devices in a mesh: band: 64 (over y, z), lev: 8 (over x, core).
Axes of the slice: x: 4, y: 8, z: 8, core: 2. Of those that a mesh axis runs over, the one named last changes fastest.
Arguments:
- concentration: float32 [4, 8, 128, 256], P(None, 'lev', 'band'), may hold values from 0.1 to 2
- target: float32 [4, 8, 128, 256], P(None, 'lev', 'band'), may hold values from -6 to 6
- zonal_wind: float32 [8, 128, 256], P('lev', 'band'), may hold values from -0.6 to 0.6
- merid_wind: float32 [8, 128, 256], P('lev', 'band'), may hold values from -0.6 to 0.6
- sea_mask: int32 [128, 256], P('band'), may hold values 0 or 1
- first_weight: float32 [2, 20, 128], replicated, may hold values from -1.25 to 1.25
- first_bias: float32 [2, 128], replicated, may hold values from -3 to 3
- middle_weight: float32 [2, 128, 128], replicated, may hold values from -0.5 to 0.5
- middle_bias: float32 [2, 128], replicated, may hold values from -3 to 3
- last_weight: float32 [2, 4, 128], replicated, may hold values from -0.125 to 0.125
- last_bias: float32 [2, 4], replicated, may hold values from -0.6 to 0.6
Outputs:
- final_field: float32 [4, 8, 128, 256], P(None, 'lev', 'band')
- first_weight_grad: float32 [2, 20, 128], replicated
- first_bias_grad: float32 [2, 128], replicated
- middle_weight_grad: float32 [2, 128, 128], replicated
- middle_bias_grad: float32 [2, 128], replicated
- last_weight_grad: float32 [2, 4, 128], replicated
- last_bias_grad: float32 [2, 4], replicated
Inputs may be any that keep to these rules, and one draw needn't show every extreme that they name: `sea_mask`: 1 marks a sea cell, 0 a land cell.
All inputs are finite; a program needn't handle non-finite values. No bound on the sum of `sea_mask` on one device may be relied on, other than what follows from the above.
Results may differ from a plain program's by a relative error of at most 0.00013.
Values sent between devices are 32-bit elements; how exact they have to be, the bound alone decides.
A program may use at most 64 MiB of HBM per device.

v0:
```python
import math
import jax
import jax.numpy as jnp
from jax import lax
from jax.sharding import PartitionSpec as P

STEPS = 3
stencil_base = (-1.0 / 12.0, 7.0 / 12.0, 7.0 / 12.0, -1.0 / 12.0)


def cut_along(array, direction, start, length):
    return lax.slice_in_dim(array, start, start + length, axis=direction)


def pad_along(array, direction, width):
    widths = [(0, 0)] * array.ndim
    widths[direction] = (width, width)
    return jnp.pad(array, widths)


def face_flux(network, stencil, courant, mask_low, mask_high):
    w_first, b_first, w_second, b_second, w_last, b_last = network
    face_shape = courant.shape
    columns = courant.size
    nbins = stencil.shape[1]
    features = jnp.concatenate(
        [
            stencil.reshape(4 * nbins, columns),
            courant.reshape(1, columns),
            (courant * courant).reshape(1, columns),
            mask_low.reshape(1, columns),
            mask_high.reshape(1, columns),
        ],
        0,
    )
    hidden_one = jnp.tanh(
        jnp.dot(w_first.T, features, precision=lax.Precision.HIGHEST) + b_first[:, None]
    )
    hidden_two = jnp.tanh(
        jnp.dot(w_second.T, hidden_one, precision=lax.Precision.HIGHEST) + b_second[:, None]
    )
    output = jnp.dot(w_last, hidden_two, precision=lax.Precision.HIGHEST) + b_last[:, None]
    correction = output - jnp.mean(output, 0, keepdims=True)
    weights_face = jnp.asarray(stencil_base, jnp.float32)[:, None] + correction
    face_value = jnp.sum(weights_face.reshape((4, 1) + face_shape) * stencil, 0)
    return courant[None] * face_value


def advance(network, padded, wind_padded, mask_padded, direction):
    length = padded.shape[direction] - 4
    stencil = jnp.stack([cut_along(padded, direction, offset, length + 1) for offset in range(4)])
    courant = 0.5 * (
        cut_along(wind_padded, direction - 1, 0, length + 1)
        + cut_along(wind_padded, direction - 1, 1, length + 1)
    )
    mask_low = cut_along(mask_padded, direction - 1, 0, length + 1)
    mask_high = cut_along(mask_padded, direction - 1, 1, length + 1)
    fluxes = face_flux(network, stencil, courant, mask_low, mask_high)
    centre = cut_along(padded, direction, 2, length)
    return centre - (
        cut_along(fluxes, direction, 1, length) - cut_along(fluxes, direction, 0, length)
    )


def to_columns(field):
    return lax.all_to_all(field, "band", split_axis=3, concat_axis=2, tiled=True)


def to_rows(field):
    return lax.all_to_all(field, "band", split_axis=2, concat_axis=3, tiled=True)


def on_device(
    concentration,
    target,
    zonal_wind,
    merid_wind,
    sea_mask,
    first_weight,
    first_bias,
    middle_weight,
    middle_bias,
    last_weight,
    last_bias,
):
    params = (first_weight, first_bias, middle_weight, middle_bias, last_weight, last_bias)
    zonal_net = tuple((member[0] for member in params))
    merid_net = tuple((member[1] for member in params))
    bins_here, levels_here, row_count, col_count = concentration.shape
    total_cells = (
        bins_here
        * levels_here
        * row_count
        * col_count
        * lax.axis_size("band")
        * lax.axis_size("lev")
    )
    loss_scale = 1.0 / math.sqrt(total_cells)
    sea_field = sea_mask.astype(jnp.float32)[None]
    wind_zonal = pad_along(zonal_wind, 2, 1)
    mask_zonal = pad_along(sea_field, 2, 1)
    stacked = jnp.concatenate([merid_wind, sea_field], 0)
    columns_data = lax.all_to_all(stacked, "band", split_axis=2, concat_axis=1, tiled=True)
    wind_merid = pad_along(columns_data[:levels_here], 1, 1)
    mask_merid = pad_along(columns_data[levels_here:], 1, 1)

    def zonal_sweep(network, padded):
        return advance(network, padded, wind_zonal, mask_zonal, 3)

    def merid_sweep(network, padded):
        return advance(network, padded, wind_merid, mask_merid, 2)

    pullbacks = []
    field = concentration
    for step_number in range(STEPS):
        field, zonal_back = jax.vjp(zonal_sweep, zonal_net, pad_along(field, 3, 2))
        moved, merid_back = jax.vjp(merid_sweep, merid_net, pad_along(to_columns(field), 2, 2))
        field = to_rows(moved)
        pullbacks.append((zonal_back, merid_back))
    cotangent = (field - target) * loss_scale
    sums = tuple((jnp.zeros_like(member) for member in params))
    for step_number in reversed(range(STEPS)):
        zonal_back, merid_back = pullbacks[step_number]
        merid_grads, padded_grad = merid_back(to_columns(cotangent))
        cotangent = to_rows(padded_grad[:, :, 2:-2])
        zonal_grads, padded_grad = zonal_back(cotangent)
        cotangent = padded_grad[:, :, :, 2:-2]
        step_grads = tuple(
            (
                jnp.stack([zonal_part, merid_part])
                for zonal_part, merid_part in zip(zonal_grads, merid_grads)
            )
        )
        sums = tuple((earlier + latest for earlier, latest in zip(sums, step_grads)))
    sums = lax.psum((sums[0], sums[1], sums[2], sums[3], sums[4], sums[5]), ("band", "lev"))
    return (field, sums[0], sums[1], sums[2], sums[3], sums[4], sums[5])


def solution(mesh):
    return jax.shard_map(
        on_device,
        mesh=mesh,
        in_specs=(
            P(None, "lev", "band", None),
            P(None, "lev", "band", None),
            P("lev", "band", None),
            P("lev", "band", None),
            P("band", None),
            P(),
            P(),
            P(),
            P(),
            P(),
            P(),
        ),
        out_specs=(P(None, "lev", "band", None), P(), P(), P(), P(), P(), P()),
        check_vma=False,
    )
```

profile of v0, /device:TPU:1, one launch (start us, length us, event | category | flops | bytes accessed | tf_op | source)
XLA Modules:
  0.0 649.2 jit_solution(2578516520645093349)
XLA Ops:
  9.5 17.3 %all-to-all-start.1 = ((f32[2,2,256]{1,0,2:T(2,128)}), f32[2,2,256]{1,0,2:T(2,128)S(1)}, u32[]{:S(2)}, u32[]{:S(2)}) async-start(f32[2,2,256]{1,0,2:T(2,128)} %copy.634), calls=%async_computation.1 | async-start | bytes 524288 | tf_op jit(solution)/shard_map/all_to_all | solution.py:103
  36.5 3.0 all-to-all-done.1
  39.6 9.1 %all-to-all-start = ((f32[4,1,2,256]{0,2,1,3:T(2,128)}), f32[4,1,2,256]{0,2,1,3:T(2,128)S(1)}, u32[]{:S(2)}, u32[]{:S(2)}) async-start(f32[4,1,2,256]{0,2,1,3:T(2,128)} %copy.631), calls=%async_computation | async-start | bytes 524288 | tf_op jit(solution)/shard_map/all_to_all | solution.py:66
  50.4 10.8 %all-to-all-done = f32[4,1,2,256]{0,2,1,3:T(2,128)S(1)} async-done(((f32[4,1,2,256]{0,2,1,3:T(2,128)}), f32[4,1,2,256]{0,2,1,3:T(2,128)S(1)}, u32[]{:S(2)}, u32[]{:S(2)}) %all-to-all-start) | async-done | bytes 8224 | tf_op jit(solution)/shard_map/all_to_all | solution.py:66
  66.5 18.4 %all_to_all.231 = f32[4,1,128,4]{3,0,1,2:T(4,128)S(1)} all-to-all(f32[4,1,128,4]{3,0,1,2:T(4,128)S(1)} %copy.642), channel_id=1, replica_groups=mesh['band'=64,'lev'=8] {'band'}, dimensions={2} | all-to-all | bytes 16384 | tf_op jit(solution)/shard_map/all_to_all | solution.py:70
  88.9 18.4 %all_to_all.232 = f32[4,1,2,256]{0,2,1,3:T(2,128)S(1)} all-to-all(f32[4,1,2,256]{0,2,1,3:T(2,128)S(1)} %copy.646), channel_id=1, replica_groups=mesh['band'=64,'lev'=8] {'band'}, dimensions={3} | all-to-all | bytes 16384 | tf_op jit(solution)/shard_map/all_to_all | solution.py:66
  110.4 1.5 concatenate.121
  111.9 1.3 fusion.8
  117.3 18.4 %all_to_all.233 = f32[4,1,128,4]{3,0,1,2:T(4,128)S(1)} all-to-all(f32[4,1,128,4]{3,0,1,2:T(4,128)S(1)} %copy.651), channel_id=1, replica_groups=mesh['band'=64,'lev'=8] {'band'}, dimensions={2} | all-to-all | bytes 16384 | tf_op jit(solution)/shard_map/all_to_all | solution.py:70
  139.6 18.4 %all_to_all.234 = f32[4,1,2,256]{0,2,1,3:T(2,128)S(1)} all-to-all(f32[4,1,2,256]{0,2,1,3:T(2,128)S(1)} %copy.655), channel_id=1, replica_groups=mesh['band'=64,'lev'=8] {'band'}, dimensions={3} | all-to-all | bytes 16384 | tf_op jit(solution)/shard_map/all_to_all | solution.py:66
  160.7 1.5 slice_bitcast_fusion.15
  163.3 2.2 reshape.1580
  165.5 2.7 concatenate.123
  168.2 1.5 fusion.6
  172.7 1.3 add_bitcast_fusion
  174.0 1.6 mul.546
  175.5 1.9 multiply_reduce_fusion
  177.4 1.7 copy.716
  179.9 1.4 fusion.44
  181.2 1.6 copy.660
  182.8 18.8 %all_to_all.235 = f32[4,1,128,4]{3,0,1,2:T(4,128)S(1)} all-to-all(f32[4,1,128,4]{3,0,1,2:T(4,128)} %copy.660), channel_id=1, replica_groups=mesh['band'=64,'lev'=8] {'band'}, dimensions={2} | all-to-all | bytes 16384 | tf_op jit(solution)/shard_map/all_to_all | solution.py:70
  202.4 1.7 all_to_all.193
  205.5 1.6 copy.664
  207.0 18.1 %all_to_all.236 = f32[4,1,2,256]{0,2,1,3:T(2,128)} all-to-all(f32[4,1,2,256]{0,2,1,3:T(2,128)} %copy.664), channel_id=1, replica_groups=mesh['band'=64,'lev'=8] {'band'}, dimensions={3} | all-to-all | bytes 16384 | tf_op jit(solution)/shard_map/all_to_all | solution.py:66
  225.2 2.6 copy.711
  227.8 1.9 copy.666
  229.7 1.7 copy.667
  232.0 1.4 multiply_bitcast_fusion.2
  233.4 1.6 copy.669
  235.0 1.9 multiply_reduce_fusion.7
  237.6 1.7 reshape.1587
  239.3 1.6 fusion.90
  242.2 1.3 convolution_bitcast_fusion.4
  250.9 4.7 all-to-all-start.8
  255.6 1.5 convolution_bitcast_fusion.21
  257.2 11.0 %all-to-all-done.8 = f32[4,1,128,4]{3,0,1,2:T(4,128)S(1)} async-done(((f32[4,1,128,4]{3,0,1,2:T(4,128)}), f32[4,1,128,4]{3,0,1,2:T(4,128)S(1)}, u32[]{:S(2)}, u32[]{:S(2)}) %all-to-all-start.8) | async-done | bytes 8224 | tf_op jit(solution)/shard_map/all_to_all | solution.py:70
  275.7 5.0 all-to-all-start.9
  281.5 11.8 %all-to-all-done.9 = f32[4,1,2,256]{0,2,1,3:T(2,128)S(1)} async-done(((f32[4,1,2,256]{0,2,1,3:T(2,128)}), f32[4,1,2,256]{0,2,1,3:T(2,128)S(1)}, u32[]{:S(2)}, u32[]{:S(2)}) %all-to-all-start.9) | async-done | bytes 8224 | tf_op jit(solution)/shard_map/all_to_all | solution.py:66
  299.1 1.3 convolution_bitcast_fusion.2
  305.4 4.7 all-to-all-start.10
  310.4 12.3 %all-to-all-done.10 = f32[4,1,128,4]{3,0,1,2:T(4,128)S(1)} async-done(((f32[4,1,128,4]{3,0,1,2:T(4,128)}), f32[4,1,128,4]{3,0,1,2:T(4,128)S(1)}, u32[]{:S(2)}, u32[]{:S(2)}) %all-to-all-start.10) | async-done | bytes 8224 | tf_op jit(solution)/shard_map/all_to_all | solution.py:70
  327.3 4.8 all-to-all-start.11
  332.3 12.3 %all-to-all-done.11 = f32[4,1,2,256]{0,2,1,3:T(2,128)S(1)} async-done(((f32[4,1,2,256]{0,2,1,3:T(2,128)}), f32[4,1,2,256]{0,2,1,3:T(2,128)S(1)}, u32[]{:S(2)}, u32[]{:S(2)}) %all-to-all-start.11) | async-done | bytes 8224 | tf_op jit(solution)/shard_map/all_to_all | solution.py:66
  351.7 4.7 all-to-all-start.12
  356.7 12.2 %all-to-all-done.12 = f32[4,1,128,4]{3,0,1,2:T(4,128)S(1)} async-done(((f32[4,1,128,4]{3,0,1,2:T(4,128)}), f32[4,1,128,4]{3,0,1,2:T(4,128)S(1)}, u32[]{:S(2)}, u32[]{:S(2)}) %all-to-all-start.12) | async-done | bytes 8224 | tf_op jit(solution)/shard_map/all_to_all | solution.py:70
  373.4 104.7 %all-reduce.47 = (f32[2,20,128]{2,1,0:T(8,128)S(1)}, f32[2,128]{1,0:T(2,128)}, f32[2,128]{1,0:T(2,128)}, f32[2,4,128]{2,1,0:T(4,128)}, f32[2,4]{1,0:T(2,128)}) all-reduce(f32[2,20,128]{2,1,0:T(8,128)S(1)} %fusion.37, f32[2,128]{1,0:T(2,128)S(1)} %get-tuple-element.216, ...), channel_id=1, replica_groups=mesh['band'=64,'lev'=8] {'band','lev'}, use_global_device_ids=true, to_apply=%region_24.25 | all-reduce | flops 6664 | bytes 53312 | tf_op jit(solution)/shard_map/psum | solution.py:135
  478.7 161.8 %all-reduce.50.cloned.1.call-done = f32[2,128,128]{2,1,0:T(8,128)} async-done(((f32[2,128,128]{2,1,0:T(8,128)}), f32[2,128,128]{2,1,0:T(8,128)}) %all-reduce.50.cloned.1.call-update) | async-done | bytes 131088 | tf_op jit(solution)/shard_map/psum | solution.py:135
  640.6 1.6 copy.764
  (493 shorter events, 88.1 us)
Async XLA Ops:
  7.2 26.5 %copy-start = (f32[2,128,128]{2,1,0:T(8,128)S(1)}, f32[2,128,128]{2,1,0:T(8,128)}, u32[]{:S(2)}) copy-start(f32[2,128,128]{2,1,0:T(8,128)} %param.24) | copy-start | bytes 393220
  8.6 26.4 %copy-start.73 = (f32[2,4,128]{2,1,0:T(4,128)S(1)}, f32[2,4,128]{2,1,0:T(4,128)}, u32[]{:S(2)}) copy-start(f32[2,4,128]{2,1,0:T(4,128)} %param.26) | copy-start | bytes 12292
  9.5 25.9 %copy-start.100 = (f32[4]{0:T(128)S(1)}, f32[4]{0:T(128)}, u32[]{:S(2)}) copy-start(f32[4]{0:T(128)} %constant.29.clone) | copy-start | bytes 52
  9.5 26.1 %copy-start.82 = (f32[4,1,2,256]{3,2,1,0:T(2,128)S(1)}, f32[4,1,2,256]{3,2,1,0:T(2,128)}, u32[]{:S(2)}) copy-start(f32[4,1,2,256]{3,2,1,0:T(2,128)} %param.17) | copy-start | bytes 24580
  9.5 30.1 %all-to-all-start.1 = ((f32[2,2,256]{1,0,2:T(2,128)}), f32[2,2,256]{1,0,2:T(2,128)S(1)}, u32[]{:S(2)}, u32[]{:S(2)}) async-start(f32[2,2,256]{1,0,2:T(2,128)} %copy.634), calls=%async_computation.1 | async-start | bytes 524288 | tf_op jit(solution)/shard_map/all_to_all | solution.py:103
  29.1 34.0 %copy-start.103 = (f32[128]{0:T(128)}, f32[128]{0:T(128)S(1)}, u32[]{:S(2)}) copy-start(f32[128]{0:T(128)S(1)} %get-tuple-element.178) | copy-start | bytes 1540
  29.1 56.4 %copy-start.105 = (f32[128]{0:T(128)}, f32[128]{0:T(128)S(1)}, u32[]{:S(2)}) copy-start(f32[128]{0:T(128)S(1)} %get-tuple-element.179) | copy-start | bytes 1540
  29.9 34.0 %copy-start.111 = (f32[128]{0:T(128)}, f32[128]{0:T(128)S(1)}, u32[]{:S(2)}) copy-start(f32[128]{0:T(128)S(1)} %get-tuple-element.176) | copy-start | bytes 1540
  29.9 56.3 %copy-start.112 = (f32[128]{0:T(128)}, f32[128]{0:T(128)S(1)}, u32[]{:S(2)}) copy-start(f32[128]{0:T(128)S(1)} %get-tuple-element.177) | copy-start | bytes 1540
  30.6 33.8 %copy-start.104 = (f32[4]{0:T(128)}, f32[4]{0:T(128)S(1)}, u32[]{:S(2)}) copy-start(f32[4]{0:T(128)S(1)} %get-tuple-element.174) | copy-start | bytes 52
  30.6 56.1 %copy-start.107 = (f32[4]{0:T(128)}, f32[4]{0:T(128)S(1)}, u32[]{:S(2)}) copy-start(f32[4]{0:T(128)S(1)} %get-tuple-element.175) | copy-start | bytes 52
  30.7 54.7 %copy-start.91 = (f32[1,514]{1,0:T(1,128)}, f32[1,514]{1,0:T(1,128)S(1)}, u32[]{:S(2)}) copy-start(f32[1,514]{1,0:T(1,128)S(1)} %reshape.1571) | copy-start | bytes 6172
  30.8 54.6 %copy-start.93 = (f32[1,514]{1,0:T(1,128)}, f32[1,514]{1,0:T(1,128)S(1)}, u32[]{:S(2)}) copy-start(f32[1,514]{1,0:T(1,128)S(1)} %reshape.1570) | copy-start | bytes 6172
  31.7 53.7 %copy-start.95 = (f32[1,514]{1,0:T(1,128)}, f32[1,514]{1,0:T(1,128)S(1)}, u32[]{:S(2)}) copy-start(f32[1,514]{1,0:T(1,128)S(1)} %reshape.1569) | copy-start | bytes 6172
  31.8 53.6 %copy-start.97 = (f32[1,514]{1,0:T(1,128)}, f32[1,514]{1,0:T(1,128)S(1)}, u32[]{:S(2)}) copy-start(f32[1,514]{1,0:T(1,128)S(1)} %reshape.1568) | copy-start | bytes 6172
  32.7 52.8 %copy-start.43 = (f32[1,20,128]{2,0,1:T(1,128)}, f32[1,20,128]{2,0,1:T(1,128)S(1)}, u32[]{:S(2)}) copy-start(f32[1,20,128]{2,0,1:T(1,128)S(1)} %get-tuple-element.154) | copy-start | bytes 30724
  39.6 21.6 %all-to-all-start = ((f32[4,1,2,256]{0,2,1,3:T(2,128)}), f32[4,1,2,256]{0,2,1,3:T(2,128)S(1)}, u32[]{:S(2)}, u32[]{:S(2)}) async-start(f32[4,1,2,256]{0,2,1,3:T(2,128)} %copy.631), calls=%async_computation | async-start | bytes 524288 | tf_op jit(solution)/shard_map/all_to_all | solution.py:66
  116.6 19.5 %copy-start.92 = (f32[1,514]{1,0:T(1,128)S(1)}, f32[1,514]{1,0:T(1,128)}, u32[]{:S(2)}) copy-start(f32[1,514]{1,0:T(1,128)} %copy-done.91) | copy-start | bytes 6172
  116.6 19.5 %copy-start.94 = (f32[1,514]{1,0:T(1,128)S(1)}, f32[1,514]{1,0:T(1,128)}, u32[]{:S(2)}) copy-start(f32[1,514]{1,0:T(1,128)} %copy-done.93) | copy-start | bytes 6172
  116.7 19.5 %copy-start.96 = (f32[1,514]{1,0:T(1,128)S(1)}, f32[1,514]{1,0:T(1,128)}, u32[]{:S(2)}) copy-start(f32[1,514]{1,0:T(1,128)} %copy-done.95) | copy-start | bytes 6172
  116.7 19.5 %copy-start.98 = (f32[1,514]{1,0:T(1,128)S(1)}, f32[1,514]{1,0:T(1,128)}, u32[]{:S(2)}) copy-start(f32[1,514]{1,0:T(1,128)} %copy-done.97) | copy-start | bytes 6172
  116.7 19.5 %copy-start.44 = (f32[1,20,128]{2,0,1:T(1,128)S(1)}, f32[1,20,128]{2,0,1:T(1,128)}, u32[]{:S(2)}) copy-start(f32[1,20,128]{2,0,1:T(1,128)} %copy-done.43) | copy-start | bytes 30724
  116.7 19.5 %copy-start.106 = (f32[128]{0:T(128)S(1)}, f32[128]{0:T(128)}, u32[]{:S(2)}) copy-start(f32[128]{0:T(128)} %copy-done.105) | copy-start | bytes 1540
  117.1 19.8 %copy-start.113 = (f32[128]{0:T(128)S(1)}, f32[128]{0:T(128)}, u32[]{:S(2)}) copy-start(f32[128]{0:T(128)} %copy-done.112) | copy-start | bytes 1540
  249.9 18.6 %copy-start.66 = (f32[1,4,1,2,257]{4,3,1,2,0:T(2,128)S(1)}, f32[1,4,1,2,257]{4,3,1,2,0:T(2,128)}, u32[]{:S(2)}) copy-start(f32[1,4,1,2,257]{4,3,1,2,0:T(2,128)} %copy-done.65) | copy-start | bytes 24676
  249.9 18.6 %copy-start.68 = (f32[1,4,1,2,257]{4,3,1,2,0:T(2,128)S(1)}, f32[1,4,1,2,257]{4,3,1,2,0:T(2,128)}, u32[]{:S(2)}) copy-start(f32[1,4,1,2,257]{4,3,1,2,0:T(2,128)} %copy-done.67) | copy-start | bytes 24676
  249.9 18.6 %copy-start.70 = (f32[1,4,1,2,257]{4,3,1,2,0:T(2,128)S(1)}, f32[1,4,1,2,257]{4,3,1,2,0:T(2,128)}, u32[]{:S(2)}) copy-start(f32[1,4,1,2,257]{4,3,1,2,0:T(2,128)} %copy-done.69) | copy-start | bytes 24676
  250.0 18.6 %copy-start.72 = (f32[1,4,1,2,257]{4,3,1,2,0:T(2,128)S(1)}, f32[1,4,1,2,257]{4,3,1,2,0:T(2,128)}, u32[]{:S(2)}) copy-start(f32[1,4,1,2,257]{4,3,1,2,0:T(2,128)} %copy-done.71) | copy-start | bytes 24676
  250.0 19.6 %copy-start.10 = (f32[514,128]{1,0:T(8,128)S(1)}, f32[514,128]{1,0:T(8,128)}, u32[]{:S(2)}) copy-start(f32[514,128]{1,0:T(8,128)} %copy-done.9) | copy-start | bytes 789508
  250.0 19.6 %copy-start.76 = (f32[2,4,128]{2,1,0:T(4,128)S(1)}, f32[2,4,128]{2,1,0:T(4,128)}, u32[]{:S(2)}) copy-start(f32[2,4,128]{2,1,0:T(4,128)} %param.26) | copy-start | bytes 12292
  250.9 19.9 %copy-start.23 = (f32[514,128]{1,0:T(8,128)S(1)}, f32[514,128]{1,0:T(8,128)}, u32[]{:S(2)}) copy-start(f32[514,128]{1,0:T(8,128)} %copy-done.22) | copy-start | bytes 789508
  250.9 17.3 %all-to-all-start.8 = ((f32[4,1,128,4]{3,0,1,2:T(4,128)}), f32[4,1,128,4]{3,0,1,2:T(4,128)S(1)}, u32[]{:S(2)}, u32[]{:S(2)}) async-start(f32[4,1,128,4]{3,0,1,2:T(4,128)} %copy.671), calls=%async_computation.8 | async-start | bytes 524288 | tf_op jit(solution)/shard_map/all_to_all | solution.py:70
  275.7 17.6 %all-to-all-start.9 = ((f32[4,1,2,256]{0,2,1,3:T(2,128)}), f32[4,1,2,256]{0,2,1,3:T(2,128)S(1)}, u32[]{:S(2)}, u32[]{:S(2)}) async-start(f32[4,1,2,256]{0,2,1,3:T(2,128)} %copy.677), calls=%async_computation.9 | async-start | bytes 524288 | tf_op jit(solution)/shard_map/all_to_all | solution.py:66
  304.4 18.6 %copy-start.58 = (f32[1,4,1,2,257]{4,3,1,2,0:T(2,128)S(1)}, f32[1,4,1,2,257]{4,3,1,2,0:T(2,128)}, u32[]{:S(2)}) copy-start(f32[1,4,1,2,257]{4,3,1,2,0:T(2,128)} %copy-done.57) | copy-start | bytes 24676
  304.4 18.6 %copy-start.60 = (f32[1,4,1,2,257]{4,3,1,2,0:T(2,128)S(1)}, f32[1,4,1,2,257]{4,3,1,2,0:T(2,128)}, u32[]{:S(2)}) copy-start(f32[1,4,1,2,257]{4,3,1,2,0:T(2,128)} %copy-done.59) | copy-start | bytes 24676
  304.4 18.6 %copy-start.62 = (f32[1,4,1,2,257]{4,3,1,2,0:T(2,128)S(1)}, f32[1,4,1,2,257]{4,3,1,2,0:T(2,128)}, u32[]{:S(2)}) copy-start(f32[1,4,1,2,257]{4,3,1,2,0:T(2,128)} %copy-done.61) | copy-start | bytes 24676
  304.5 18.6 %copy-start.64 = (f32[1,4,1,2,257]{4,3,1,2,0:T(2,128)S(1)}, f32[1,4,1,2,257]{4,3,1,2,0:T(2,128)}, u32[]{:S(2)}) copy-start(f32[1,4,1,2,257]{4,3,1,2,0:T(2,128)} %copy-done.63) | copy-start | bytes 24676
  304.5 19.0 %copy-start.6 = (f32[514,128]{1,0:T(8,128)S(1)}, f32[514,128]{1,0:T(8,128)}, u32[]{:S(2)}) copy-start(f32[514,128]{1,0:T(8,128)} %copy-done.5) | copy-start | bytes 789508
  304.5 19.0 %copy-start.77 = (f32[2,4,128]{2,1,0:T(4,128)S(1)}, f32[2,4,128]{2,1,0:T(4,128)}, u32[]{:S(2)}) copy-start(f32[2,4,128]{2,1,0:T(4,128)} %param.26) | copy-start | bytes 12292
  305.3 18.8 %copy-start.19 = (f32[514,128]{1,0:T(8,128)S(1)}, f32[514,128]{1,0:T(8,128)}, u32[]{:S(2)}) copy-start(f32[514,128]{1,0:T(8,128)} %copy-done.18) | copy-start | bytes 789508
  305.4 17.3 %all-to-all-start.10 = ((f32[4,1,128,4]{3,0,1,2:T(4,128)}), f32[4,1,128,4]{3,0,1,2:T(4,128)S(1)}, u32[]{:S(2)}, u32[]{:S(2)}) async-start(f32[4,1,128,4]{3,0,1,2:T(4,128)} %copy.684), calls=%async_computation.10 | async-start | bytes 524288 | tf_op jit(solution)/shard_map/all_to_all | solution.py:70
  327.3 17.3 %all-to-all-start.11 = ((f32[4,1,2,256]{0,2,1,3:T(2,128)}), f32[4,1,2,256]{0,2,1,3:T(2,128)S(1)}, u32[]{:S(2)}, u32[]{:S(2)}) async-start(f32[4,1,2,256]{0,2,1,3:T(2,128)} %copy.690), calls=%async_computation.11 | async-start | bytes 524288 | tf_op jit(solution)/shard_map/all_to_all | solution.py:66
  350.7 18.5 %copy-start.50 = (f32[1,4,1,2,257]{4,3,1,2,0:T(2,128)S(1)}, f32[1,4,1,2,257]{4,3,1,2,0:T(2,128)}, u32[]{:S(2)}) copy-start(f32[1,4,1,2,257]{4,3,1,2,0:T(2,128)} %copy-done.49) | copy-start | bytes 24676
  350.7 18.5 %copy-start.52 = (f32[1,4,1,2,257]{4,3,1,2,0:T(2,128)S(1)}, f32[1,4,1,2,257]{4,3,1,2,0:T(2,128)}, u32[]{:S(2)}) copy-start(f32[1,4,1,2,257]{4,3,1,2,0:T(2,128)} %copy-done.51) | copy-start | bytes 24676
  350.8 19.0 %copy-start.2 = (f32[514,128]{1,0:T(8,128)S(1)}, f32[514,128]{1,0:T(8,128)}, u32[]{:S(2)}) copy-start(f32[514,128]{1,0:T(8,128)} %copy-done.1) | copy-start | bytes 789508
  351.7 18.8 %copy-start.15 = (f32[514,128]{1,0:T(8,128)S(1)}, f32[514,128]{1,0:T(8,128)}, u32[]{:S(2)}) copy-start(f32[514,128]{1,0:T(8,128)} %copy-done.14) | copy-start | bytes 789508
  351.7 17.3 %all-to-all-start.12 = ((f32[4,1,128,4]{3,0,1,2:T(4,128)}), f32[4,1,128,4]{3,0,1,2:T(4,128)S(1)}, u32[]{:S(2)}, u32[]{:S(2)}) async-start(f32[4,1,128,4]{3,0,1,2:T(4,128)} %copy.697), calls=%async_computation.12 | async-start | bytes 524288 | tf_op jit(solution)/shard_map/all_to_all | solution.py:70
  356.4 284.2 %all-reduce.50.cloned.1.call-start = ((), (), s32[]{:S(2)}) async-start(), calls=%async_computation.13 | async-start | bytes 262144 | tf_op jit(solution)/shard_map/psum | solution.py:135
  (83 other events, 296.6 us)
Sparse Core Ops, SparseCore 0:
  373.0 267.4 all-reduce.49
where the time goes:
time: 660 us; the launch traced here: 649 us
  waiting for transfers between devices  235 us (36%)
  blocking collectives  215 us (33%)
  local copies, waits for them, and re-layouts  70 us (11%)
  starting transfers between devices  50.5 us (8%)
  matrix products  39.1 us (6%)
  other arithmetic  22.5 us (3%)
  between operations  16.6 us (3%)
    psum x1, waiting for transfers between devices, on_device(): lax.psum((sums[0], sums[1], sums[2], sums[3], sums[4], sums[5]), ('band',...  162 us
    psum x1, blocking collectives, on_device(): lax.psum((sums[0], sums[1], sums[2], sums[3], sums[4], sums[5]), ('band',...  105 us
    all_to_all x3, blocking collectives, to_rows(): lax.all_to_all(field, 'band', split_axis=2, concat_axis=3, tiled=True)  55.7 us
    all_to_all x3, blocking collectives, to_columns(): lax.all_to_all(field, 'band', split_axis=3, concat_axis=2, tiled=True)  54.9 us
    all_to_all x3, waiting for transfers between devices, to_rows(): lax.all_to_all(field, 'band', split_axis=2, concat_axis=3, tiled=True)  35.5 us
    all_to_all x3, waiting for transfers between devices, to_columns(): lax.all_to_all(field, 'band', split_axis=3, concat_axis=2, tiled=True)  34.8 us
    all_to_all x3, starting transfers between devices, to_columns(): lax.all_to_all(field, 'band', split_axis=3, concat_axis=2, tiled=True)  18.9 us
    all_to_all x1, starting transfers between devices, on_device(): lax.all_to_all(stacked, 'band', split_axis=2, concat_axis=1, tiled=True)  17.3 us
  transfers between devices with their start and end apart: 8, of which 8 were waited for; matrix products, arithmetic and copies ran while one was open for 2% of the time, Pallas kernels for 0%

commit v1 on v0

--- a/solution.py
+++ b/solution.py
@@ -132,7 +132,13 @@
             )
         )
         sums = tuple((earlier + latest for earlier, latest in zip(sums, step_grads)))
-    sums = lax.psum((sums[0], sums[1], sums[2], sums[3], sums[4], sums[5]), ("band", "lev"))
+
+    def put_results_all(message, named_axis, ax_name):
+        for j in (named_axis, ax_name):
+            message = lax.psum(message, j)
+        return message
+
+    sums = put_results_all((sums[0], sums[1], sums[2], sums[3], sums[4], sums[5]), "band", "lev")
     return (field, sums[0], sums[1], sums[2], sums[3], sums[4], sums[5])
 
 

time: 660 us -> 845 us (1.28)
  blocking collectives: 215 us -> 413 us
  waiting for transfers between devices: 235 us -> 223 us
    psum x1 -> x2, blocking collectives: 105 us -> 303 us  [put_results_all(): message = lax.psum(message, j)]
    psum x1 -> x2, waiting for transfers between devices: 162 us -> 149 us  [put_results_all(): message = lax.psum(message, j)]
  transfers between devices with their start and end apart: 8 -> 9, of which waited for: 8 -> 8; matrix products, arithmetic and copies ran while one was open for 2% -> 2% of each run, Pallas kernels for 0% -> 0%
where the time goes in v1:
time: 845 us; the launch traced here: 834 us
  blocking collectives  413 us (49%)
  waiting for transfers between devices  223 us (26%)
  local copies, waits for them, and re-layouts  69.3 us (8%)
  starting transfers between devices  49.8 us (6%)
  matrix products  39.2 us (5%)
  other arithmetic  22.5 us (3%)
  between operations  16.6 us (2%)
    psum x2, blocking collectives, put_results_all(): message = lax.psum(message, j)  303 us
    psum x2, waiting for transfers between devices, put_results_all(): message = lax.psum(message, j)  149 us
    all_to_all x3, blocking collectives, to_rows(): lax.all_to_all(field, 'band', split_axis=2, concat_axis=3, tiled=True)  55.7 us
    all_to_all x3, blocking collectives, to_columns(): lax.all_to_all(field, 'band', split_axis=3, concat_axis=2, tiled=True)  54.9 us
    all_to_all x3, waiting for transfers between devices, to_rows(): lax.all_to_all(field, 'band', split_axis=2, concat_axis=3, tiled=True)  35.5 us
    all_to_all x3, waiting for transfers between devices, to_columns(): lax.all_to_all(field, 'band', split_axis=3, concat_axis=2, tiled=True)  34.8 us
    all_to_all x3, starting transfers between devices, to_columns(): lax.all_to_all(field, 'band', split_axis=3, concat_axis=2, tiled=True)  18.2 us
    all_to_all x1, starting transfers between devices, on_device(): lax.all_to_all(stacked, 'band', split_axis=2, concat_axis=1, tiled=True)  17.3 us
  transfers between devices with their start and end apart: 9, of which 8 were waited for; matrix products, arithmetic and copies ran while one was open for 2% of the time, Pallas kernels for 0%

profile of v1, /device:TPU:1, one launch (start us, length us, event | category | flops | bytes accessed | tf_op | source)
XLA Modules:
  0.0 833.8 jit_solution(6127829722203833983)
XLA Ops:
  9.5 17.3 %all-to-all-start.1 = ((f32[2,2,256]{1,0,2:T(2,128)}), f32[2,2,256]{1,0,2:T(2,128)S(1)}, u32[]{:S(2)}, u32[]{:S(2)}) async-start(f32[2,2,256]{1,0,2:T(2,128)} %copy.634), calls=%async_computation.1 | async-start | bytes 524288 | tf_op jit(solution)/shard_map/all_to_all | solution.py:103
  35.8 3.7 all-to-all-done.1
  39.6 8.4 %all-to-all-start = ((f32[4,1,2,256]{0,2,1,3:T(2,128)}), f32[4,1,2,256]{0,2,1,3:T(2,128)S(1)}, u32[]{:S(2)}, u32[]{:S(2)}) async-start(f32[4,1,2,256]{0,2,1,3:T(2,128)} %copy.631), calls=%async_computation | async-start | bytes 524288 | tf_op jit(solution)/shard_map/all_to_all | solution.py:66
  49.7 10.8 %all-to-all-done = f32[4,1,2,256]{0,2,1,3:T(2,128)S(1)} async-done(((f32[4,1,2,256]{0,2,1,3:T(2,128)}), f32[4,1,2,256]{0,2,1,3:T(2,128)S(1)}, u32[]{:S(2)}, u32[]{:S(2)}) %all-to-all-start) | async-done | bytes 8224 | tf_op jit(solution)/shard_map/all_to_all | solution.py:66
  65.7 18.4 %all_to_all.231 = f32[4,1,128,4]{3,0,1,2:T(4,128)S(1)} all-to-all(f32[4,1,128,4]{3,0,1,2:T(4,128)S(1)} %copy.642), channel_id=1, replica_groups=mesh['band'=64,'lev'=8] {'band'}, dimensions={2} | all-to-all | bytes 16384 | tf_op jit(solution)/shard_map/all_to_all | solution.py:70
  88.2 18.4 %all_to_all.232 = f32[4,1,2,256]{0,2,1,3:T(2,128)S(1)} all-to-all(f32[4,1,2,256]{0,2,1,3:T(2,128)S(1)} %copy.646), channel_id=1, replica_groups=mesh['band'=64,'lev'=8] {'band'}, dimensions={3} | all-to-all | bytes 16384 | tf_op jit(solution)/shard_map/all_to_all | solution.py:66
  109.6 1.5 concatenate.121
  111.2 1.3 fusion.8
  116.6 18.4 %all_to_all.233 = f32[4,1,128,4]{3,0,1,2:T(4,128)S(1)} all-to-all(f32[4,1,128,4]{3,0,1,2:T(4,128)S(1)} %copy.651), channel_id=1, replica_groups=mesh['band'=64,'lev'=8] {'band'}, dimensions={2} | all-to-all | bytes 16384 | tf_op jit(solution)/shard_map/all_to_all | solution.py:70
  138.9 18.4 %all_to_all.234 = f32[4,1,2,256]{0,2,1,3:T(2,128)S(1)} all-to-all(f32[4,1,2,256]{0,2,1,3:T(2,128)S(1)} %copy.655), channel_id=1, replica_groups=mesh['band'=64,'lev'=8] {'band'}, dimensions={3} | all-to-all | bytes 16384 | tf_op jit(solution)/shard_map/all_to_all | solution.py:66
  160.0 1.5 slice_bitcast_fusion.15
  162.6 2.2 reshape.1580
  164.8 2.7 concatenate.123
  167.5 1.5 fusion.6
  173.3 1.6 mul.546
  174.9 1.9 multiply_reduce_fusion
  176.7 1.7 copy.716
  179.2 1.4 fusion.44
  180.6 1.6 copy.660
  182.1 18.8 %all_to_all.235 = f32[4,1,128,4]{3,0,1,2:T(4,128)S(1)} all-to-all(f32[4,1,128,4]{3,0,1,2:T(4,128)} %copy.660), channel_id=1, replica_groups=mesh['band'=64,'lev'=8] {'band'}, dimensions={2} | all-to-all | bytes 16384 | tf_op jit(solution)/shard_map/all_to_all | solution.py:70
  201.8 1.7 all_to_all.193
  204.8 1.6 copy.664
  206.3 18.1 %all_to_all.236 = f32[4,1,2,256]{0,2,1,3:T(2,128)} all-to-all(f32[4,1,2,256]{0,2,1,3:T(2,128)} %copy.664), channel_id=1, replica_groups=mesh['band'=64,'lev'=8] {'band'}, dimensions={3} | all-to-all | bytes 16384 | tf_op jit(solution)/shard_map/all_to_all | solution.py:66
  224.5 2.7 copy.711
  227.1 1.9 copy.666
  229.0 1.7 copy.667
  231.4 1.4 multiply_bitcast_fusion.2
  232.7 1.6 copy.669
  234.3 1.9 multiply_reduce_fusion.7
  236.9 1.7 reshape.1587
  238.6 1.6 fusion.90
  241.6 1.3 convolution_bitcast_fusion.4
  250.2 4.8 all-to-all-start.8
  255.0 1.5 convolution_bitcast_fusion.21
  256.5 11.0 %all-to-all-done.8 = f32[4,1,128,4]{3,0,1,2:T(4,128)S(1)} async-done(((f32[4,1,128,4]{3,0,1,2:T(4,128)}), f32[4,1,128,4]{3,0,1,2:T(4,128)S(1)}, u32[]{:S(2)}, u32[]{:S(2)}) %all-to-all-start.8) | async-done | bytes 8224 | tf_op jit(solution)/shard_map/all_to_all | solution.py:70
  270.1 1.3 convolution_bitcast_fusion.5
  275.0 5.0 all-to-all-start.9
  280.9 11.8 %all-to-all-done.9 = f32[4,1,2,256]{0,2,1,3:T(2,128)S(1)} async-done(((f32[4,1,2,256]{0,2,1,3:T(2,128)}), f32[4,1,2,256]{0,2,1,3:T(2,128)S(1)}, u32[]{:S(2)}, u32[]{:S(2)}) %all-to-all-start.9) | async-done | bytes 8224 | tf_op jit(solution)/shard_map/all_to_all | solution.py:66
  304.7 4.7 all-to-all-start.10
  309.7 12.3 %all-to-all-done.10 = f32[4,1,128,4]{3,0,1,2:T(4,128)S(1)} async-done(((f32[4,1,128,4]{3,0,1,2:T(4,128)}), f32[4,1,128,4]{3,0,1,2:T(4,128)S(1)}, u32[]{:S(2)}, u32[]{:S(2)}) %all-to-all-start.10) | async-done | bytes 8224 | tf_op jit(solution)/shard_map/all_to_all | solution.py:70
  326.6 4.8 all-to-all-start.11
  331.6 12.3 %all-to-all-done.11 = f32[4,1,2,256]{0,2,1,3:T(2,128)S(1)} async-done(((f32[4,1,2,256]{0,2,1,3:T(2,128)}), f32[4,1,2,256]{0,2,1,3:T(2,128)S(1)}, u32[]{:S(2)}, u32[]{:S(2)}) %all-to-all-start.11) | async-done | bytes 8224 | tf_op jit(solution)/shard_map/all_to_all | solution.py:66
  351.0 4.8 all-to-all-start.12
  356.1 12.2 %all-to-all-done.12 = f32[4,1,128,4]{3,0,1,2:T(4,128)S(1)} async-done(((f32[4,1,128,4]{3,0,1,2:T(4,128)}), f32[4,1,128,4]{3,0,1,2:T(4,128)S(1)}, u32[]{:S(2)}, u32[]{:S(2)}) %all-to-all-start.12) | async-done | bytes 8224 | tf_op jit(solution)/shard_map/all_to_all | solution.py:70
  372.7 149.0 %all-reduce.52.cloned.1.call-done = f32[2,128,128]{2,1,0:T(8,128)} async-done(((f32[2,128,128]{2,1,0:T(8,128)}), f32[2,128,128]{2,1,0:T(8,128)}) %all-reduce.52.cloned.1.call-update) | async-done | bytes 131088 | tf_op jit(solution)/shard_map/psum | solution.py:138
  521.8 222.1 %all-reduce.47 = (f32[2,20,128]{2,1,0:T(8,128)S(1)}, f32[2,128]{1,0:T(2,128)S(1)}, f32[2,128]{1,0:T(2,128)S(1)}, f32[2,4,128]{2,1,0:T(4,128)S(1)}, f32[2,4]{1,0:T(2,128)S(1)}) all-reduce(f32[2,20,128]{2,1,0:T(8,128)S(1)} %fusion.37, f32[2,128]{1,0:T(2,128)S(1)} %get-tuple-element.221, ...), channel_id=1, replica_groups=mesh['band'=64,'lev'=8] {'band'}, use_global_device_ids=true, to_apply=%region_24.25 | all-reduce | flops 6664 | bytes 53312 | tf_op jit(solution)/shard_map/psum | solution.py:138
  743.9 80.7 %all-reduce.48 = (f32[2,20,128]{2,1,0:T(8,128)S(1)}, f32[2,128]{1,0:T(2,128)}, f32[2,128]{1,0:T(2,128)}, f32[2,4,128]{2,1,0:T(4,128)}, f32[2,4]{1,0:T(2,128)}) all-reduce(f32[2,20,128]{2,1,0:T(8,128)S(1)} %get-tuple-element.96, f32[2,128]{1,0:T(2,128)S(1)} %get-tuple-element.97, ...), channel_id=1, replica_groups=mesh['band'=64,'lev'=8] {'lev'}, use_global_device_ids=true, to_apply=%region_25.26 | all-reduce | flops 6664 | bytes 53312 | tf_op jit(solution)/shard_map/psum | solution.py:138
  825.2 1.6 copy.765
  (497 shorter events, 88.8 us)
Async XLA Ops:
  7.2 26.5 %copy-start = (f32[2,128,128]{2,1,0:T(8,128)S(1)}, f32[2,128,128]{2,1,0:T(8,128)}, u32[]{:S(2)}) copy-start(f32[2,128,128]{2,1,0:T(8,128)} %param.24) | copy-start | bytes 393220
  8.6 25.7 %copy-start.73 = (f32[2,4,128]{2,1,0:T(4,128)S(1)}, f32[2,4,128]{2,1,0:T(4,128)}, u32[]{:S(2)}) copy-start(f32[2,4,128]{2,1,0:T(4,128)} %param.26) | copy-start | bytes 12292
  9.5 25.2 %copy-start.100 = (f32[4]{0:T(128)S(1)}, f32[4]{0:T(128)}, u32[]{:S(2)}) copy-start(f32[4]{0:T(128)} %constant.29.clone) | copy-start | bytes 52
  9.5 25.4 %copy-start.82 = (f32[4,1,2,256]{3,2,1,0:T(2,128)S(1)}, f32[4,1,2,256]{3,2,1,0:T(2,128)}, u32[]{:S(2)}) copy-start(f32[4,1,2,256]{3,2,1,0:T(2,128)} %param.17) | copy-start | bytes 24580
  9.5 30.1 %all-to-all-start.1 = ((f32[2,2,256]{1,0,2:T(2,128)}), f32[2,2,256]{1,0,2:T(2,128)S(1)}, u32[]{:S(2)}, u32[]{:S(2)}) async-start(f32[2,2,256]{1,0,2:T(2,128)} %copy.634), calls=%async_computation.1 | async-start | bytes 524288 | tf_op jit(solution)/shard_map/all_to_all | solution.py:103
  29.1 33.3 %copy-start.103 = (f32[128]{0:T(128)}, f32[128]{0:T(128)S(1)}, u32[]{:S(2)}) copy-start(f32[128]{0:T(128)S(1)} %get-tuple-element.183) | copy-start | bytes 1540
  29.1 55.6 %copy-start.105 = (f32[128]{0:T(128)}, f32[128]{0:T(128)S(1)}, u32[]{:S(2)}) copy-start(f32[128]{0:T(128)S(1)} %get-tuple-element.184) | copy-start | bytes 1540
  29.9 33.2 %copy-start.111 = (f32[128]{0:T(128)}, f32[128]{0:T(128)S(1)}, u32[]{:S(2)}) copy-start(f32[128]{0:T(128)S(1)} %get-tuple-element.181) | copy-start | bytes 1540
  29.9 55.6 %copy-start.112 = (f32[128]{0:T(128)}, f32[128]{0:T(128)S(1)}, u32[]{:S(2)}) copy-start(f32[128]{0:T(128)S(1)} %get-tuple-element.182) | copy-start | bytes 1540
  30.6 33.1 %copy-start.104 = (f32[4]{0:T(128)}, f32[4]{0:T(128)S(1)}, u32[]{:S(2)}) copy-start(f32[4]{0:T(128)S(1)} %get-tuple-element.179) | copy-start | bytes 52
  30.6 55.4 %copy-start.107 = (f32[4]{0:T(128)}, f32[4]{0:T(128)S(1)}, u32[]{:S(2)}) copy-start(f32[4]{0:T(128)S(1)} %get-tuple-element.180) | copy-start | bytes 52
  30.7 54.0 %copy-start.91 = (f32[1,514]{1,0:T(1,128)}, f32[1,514]{1,0:T(1,128)S(1)}, u32[]{:S(2)}) copy-start(f32[1,514]{1,0:T(1,128)S(1)} %reshape.1571) | copy-start | bytes 6172
  30.8 53.9 %copy-start.93 = (f32[1,514]{1,0:T(1,128)}, f32[1,514]{1,0:T(1,128)S(1)}, u32[]{:S(2)}) copy-start(f32[1,514]{1,0:T(1,128)S(1)} %reshape.1570) | copy-start | bytes 6172
  31.7 53.0 %copy-start.95 = (f32[1,514]{1,0:T(1,128)}, f32[1,514]{1,0:T(1,128)S(1)}, u32[]{:S(2)}) copy-start(f32[1,514]{1,0:T(1,128)S(1)} %reshape.1569) | copy-start | bytes 6172
  31.8 52.9 %copy-start.97 = (f32[1,514]{1,0:T(1,128)}, f32[1,514]{1,0:T(1,128)S(1)}, u32[]{:S(2)}) copy-start(f32[1,514]{1,0:T(1,128)S(1)} %reshape.1568) | copy-start | bytes 6172
  32.6 52.1 %copy-start.43 = (f32[1,20,128]{2,0,1:T(1,128)}, f32[1,20,128]{2,0,1:T(1,128)S(1)}, u32[]{:S(2)}) copy-start(f32[1,20,128]{2,0,1:T(1,128)S(1)} %get-tuple-element.159) | copy-start | bytes 30724
  39.6 20.9 %all-to-all-start = ((f32[4,1,2,256]{0,2,1,3:T(2,128)}), f32[4,1,2,256]{0,2,1,3:T(2,128)S(1)}, u32[]{:S(2)}, u32[]{:S(2)}) async-start(f32[4,1,2,256]{0,2,1,3:T(2,128)} %copy.631), calls=%async_computation | async-start | bytes 524288 | tf_op jit(solution)/shard_map/all_to_all | solution.py:66
  115.9 19.5 %copy-start.92 = (f32[1,514]{1,0:T(1,128)S(1)}, f32[1,514]{1,0:T(1,128)}, u32[]{:S(2)}) copy-start(f32[1,514]{1,0:T(1,128)} %copy-done.91) | copy-start | bytes 6172
  115.9 19.5 %copy-start.94 = (f32[1,514]{1,0:T(1,128)S(1)}, f32[1,514]{1,0:T(1,128)}, u32[]{:S(2)}) copy-start(f32[1,514]{1,0:T(1,128)} %copy-done.93) | copy-start | bytes 6172
  116.0 19.5 %copy-start.96 = (f32[1,514]{1,0:T(1,128)S(1)}, f32[1,514]{1,0:T(1,128)}, u32[]{:S(2)}) copy-start(f32[1,514]{1,0:T(1,128)} %copy-done.95) | copy-start | bytes 6172
  116.0 19.5 %copy-start.98 = (f32[1,514]{1,0:T(1,128)S(1)}, f32[1,514]{1,0:T(1,128)}, u32[]{:S(2)}) copy-start(f32[1,514]{1,0:T(1,128)} %copy-done.97) | copy-start | bytes 6172
  116.0 19.5 %copy-start.44 = (f32[1,20,128]{2,0,1:T(1,128)S(1)}, f32[1,20,128]{2,0,1:T(1,128)}, u32[]{:S(2)}) copy-start(f32[1,20,128]{2,0,1:T(1,128)} %copy-done.43) | copy-start | bytes 30724
  116.0 19.5 %copy-start.106 = (f32[128]{0:T(128)S(1)}, f32[128]{0:T(128)}, u32[]{:S(2)}) copy-start(f32[128]{0:T(128)} %copy-done.105) | copy-start | bytes 1540
  116.4 19.8 %copy-start.113 = (f32[128]{0:T(128)S(1)}, f32[128]{0:T(128)}, u32[]{:S(2)}) copy-start(f32[128]{0:T(128)} %copy-done.112) | copy-start | bytes 1540
  249.3 18.6 %copy-start.66 = (f32[1,4,1,2,257]{4,3,1,2,0:T(2,128)S(1)}, f32[1,4,1,2,257]{4,3,1,2,0:T(2,128)}, u32[]{:S(2)}) copy-start(f32[1,4,1,2,257]{4,3,1,2,0:T(2,128)} %copy-done.65) | copy-start | bytes 24676
  249.3 18.6 %copy-start.68 = (f32[1,4,1,2,257]{4,3,1,2,0:T(2,128)S(1)}, f32[1,4,1,2,257]{4,3,1,2,0:T(2,128)}, u32[]{:S(2)}) copy-start(f32[1,4,1,2,257]{4,3,1,2,0:T(2,128)} %copy-done.67) | copy-start | bytes 24676
  249.3 18.6 %copy-start.70 = (f32[1,4,1,2,257]{4,3,1,2,0:T(2,128)S(1)}, f32[1,4,1,2,257]{4,3,1,2,0:T(2,128)}, u32[]{:S(2)}) copy-start(f32[1,4,1,2,257]{4,3,1,2,0:T(2,128)} %copy-done.69) | copy-start | bytes 24676
  249.3 18.6 %copy-start.72 = (f32[1,4,1,2,257]{4,3,1,2,0:T(2,128)S(1)}, f32[1,4,1,2,257]{4,3,1,2,0:T(2,128)}, u32[]{:S(2)}) copy-start(f32[1,4,1,2,257]{4,3,1,2,0:T(2,128)} %copy-done.71) | copy-start | bytes 24676
  249.3 19.6 %copy-start.10 = (f32[514,128]{1,0:T(8,128)S(1)}, f32[514,128]{1,0:T(8,128)}, u32[]{:S(2)}) copy-start(f32[514,128]{1,0:T(8,128)} %copy-done.9) | copy-start | bytes 789508
  249.3 19.6 %copy-start.76 = (f32[2,4,128]{2,1,0:T(4,128)S(1)}, f32[2,4,128]{2,1,0:T(4,128)}, u32[]{:S(2)}) copy-start(f32[2,4,128]{2,1,0:T(4,128)} %param.26) | copy-start | bytes 12292
  250.2 19.9 %copy-start.23 = (f32[514,128]{1,0:T(8,128)S(1)}, f32[514,128]{1,0:T(8,128)}, u32[]{:S(2)}) copy-start(f32[514,128]{1,0:T(8,128)} %copy-done.22) | copy-start | bytes 789508
  250.2 17.3 %all-to-all-start.8 = ((f32[4,1,128,4]{3,0,1,2:T(4,128)}), f32[4,1,128,4]{3,0,1,2:T(4,128)S(1)}, u32[]{:S(2)}, u32[]{:S(2)}) async-start(f32[4,1,128,4]{3,0,1,2:T(4,128)} %copy.671), calls=%async_computation.8 | async-start | bytes 524288 | tf_op jit(solution)/shard_map/all_to_all | solution.py:70
  275.0 17.6 %all-to-all-start.9 = ((f32[4,1,2,256]{0,2,1,3:T(2,128)}), f32[4,1,2,256]{0,2,1,3:T(2,128)S(1)}, u32[]{:S(2)}, u32[]{:S(2)}) async-start(f32[4,1,2,256]{0,2,1,3:T(2,128)} %copy.677), calls=%async_computation.9 | async-start | bytes 524288 | tf_op jit(solution)/shard_map/all_to_all | solution.py:66
  303.8 18.6 %copy-start.58 = (f32[1,4,1,2,257]{4,3,1,2,0:T(2,128)S(1)}, f32[1,4,1,2,257]{4,3,1,2,0:T(2,128)}, u32[]{:S(2)}) copy-start(f32[1,4,1,2,257]{4,3,1,2,0:T(2,128)} %copy-done.57) | copy-start | bytes 24676
  303.8 18.6 %copy-start.60 = (f32[1,4,1,2,257]{4,3,1,2,0:T(2,128)S(1)}, f32[1,4,1,2,257]{4,3,1,2,0:T(2,128)}, u32[]{:S(2)}) copy-start(f32[1,4,1,2,257]{4,3,1,2,0:T(2,128)} %copy-done.59) | copy-start | bytes 24676
  303.8 19.0 %copy-start.6 = (f32[514,128]{1,0:T(8,128)S(1)}, f32[514,128]{1,0:T(8,128)}, u32[]{:S(2)}) copy-start(f32[514,128]{1,0:T(8,128)} %copy-done.5) | copy-start | bytes 789508
  303.8 19.0 %copy-start.77 = (f32[2,4,128]{2,1,0:T(4,128)S(1)}, f32[2,4,128]{2,1,0:T(4,128)}, u32[]{:S(2)}) copy-start(f32[2,4,128]{2,1,0:T(4,128)} %param.26) | copy-start | bytes 12292
  304.7 18.8 %copy-start.19 = (f32[514,128]{1,0:T(8,128)S(1)}, f32[514,128]{1,0:T(8,128)}, u32[]{:S(2)}) copy-start(f32[514,128]{1,0:T(8,128)} %copy-done.18) | copy-start | bytes 789508
  304.7 17.3 %all-to-all-start.10 = ((f32[4,1,128,4]{3,0,1,2:T(4,128)}), f32[4,1,128,4]{3,0,1,2:T(4,128)S(1)}, u32[]{:S(2)}, u32[]{:S(2)}) async-start(f32[4,1,128,4]{3,0,1,2:T(4,128)} %copy.684), calls=%async_computation.10 | async-start | bytes 524288 | tf_op jit(solution)/shard_map/all_to_all | solution.py:70
  326.6 17.3 %all-to-all-start.11 = ((f32[4,1,2,256]{0,2,1,3:T(2,128)}), f32[4,1,2,256]{0,2,1,3:T(2,128)S(1)}, u32[]{:S(2)}, u32[]{:S(2)}) async-start(f32[4,1,2,256]{0,2,1,3:T(2,128)} %copy.690), calls=%async_computation.11 | async-start | bytes 524288 | tf_op jit(solution)/shard_map/all_to_all | solution.py:66
  350.1 19.0 %copy-start.2 = (f32[514,128]{1,0:T(8,128)S(1)}, f32[514,128]{1,0:T(8,128)}, u32[]{:S(2)}) copy-start(f32[514,128]{1,0:T(8,128)} %copy-done.1) | copy-start | bytes 789508
  351.0 18.8 %copy-start.15 = (f32[514,128]{1,0:T(8,128)S(1)}, f32[514,128]{1,0:T(8,128)}, u32[]{:S(2)}) copy-start(f32[514,128]{1,0:T(8,128)} %copy-done.14) | copy-start | bytes 789508
  351.0 17.3 %all-to-all-start.12 = ((f32[4,1,128,4]{3,0,1,2:T(4,128)}), f32[4,1,128,4]{3,0,1,2:T(4,128)S(1)}, u32[]{:S(2)}, u32[]{:S(2)}) async-start(f32[4,1,128,4]{3,0,1,2:T(4,128)} %copy.697), calls=%async_computation.12 | async-start | bytes 524288 | tf_op jit(solution)/shard_map/all_to_all | solution.py:70
  355.8 166.0 %all-reduce.52.cloned.1.call-start = ((), (), s32[]{:S(2)}) async-start(), calls=%async_computation.13 | async-start | bytes 262144 | tf_op jit(solution)/shard_map/psum | solution.py:138
  370.6 151.2 %copy-start.120 = (f32[4]{0:T(128)S(1)}, f32[4]{0:T(128)}, u32[]{:S(2)}) copy-start(f32[4]{0:T(128)} %get-tuple-element.114) | copy-start | bytes 52
  370.6 151.2 %copy-start.121 = (f32[4]{0:T(128)S(1)}, f32[4]{0:T(128)}, u32[]{:S(2)}) copy-start(f32[4]{0:T(128)} %get-tuple-element.116) | copy-start | bytes 52
  370.6 151.2 %copy-start.122 = (f32[4]{0:T(128)S(1)}, f32[4]{0:T(128)}, u32[]{:S(2)}) copy-start(f32[4]{0:T(128)} %get-tuple-element.112) | copy-start | bytes 52
  372.3 452.9 %all-reduce.54.cloned.1.call-start = ((), (), s32[]{:S(2)}) async-start(), calls=%async_computation.14 | async-start | bytes 262144 | tf_op jit(solution)/shard_map/psum | solution.py:138
  (84 other events, 393.1 us)
Sparse Core Ops, SparseCore 0:
  372.4 149.3 all-reduce.51
  524.1 70.5 all-reduce.53
